TPU v7x, 1024 devices: a whole 4x4x32 slice. The times are simulated.
1024 devices in a mesh: gx: 32 (over x, y, core), gy: 32 (over z).
Axes of the slice: x: 4, y: 4, z: 32, core: 2. Of those that a mesh axis runs over, the one named last changes fastest.
Arguments:
- fields: float32 [4, 512, 512, 128], P(None, 'gx', 'gy'), may hold values from -6 to 6
- factor_x: float32 [512, 32], P('gx'), may hold values from -0.5 to 0.5
- factor_y: float32 [512, 32], P('gy'), may hold values from -0.5 to 0.5
Outputs:
- advanced: float32 [4, 512, 512, 128], P(None, 'gx', 'gy')
- core_tensor: float32 [4, 32, 32, 128], P(None, 'gx', 'gy')
- rebuilt: float32 [4, 512, 512, 128], P(None, 'gx', 'gy')
All inputs are finite; a program needn't handle non-finite values.
Results may differ from a plain program's by a relative error of at most 0.000082.
Values sent between devices are 32-bit elements; how exact they have to be, the bound alone decides.
A program may use at most 32 MiB of HBM per device.

v0:
```python
import math

import jax
import jax.numpy as jnp
from jax import lax
from jax.sharding import PartitionSpec as P

TIME_STEP = 0.2
REACT_RATE = 0.5
HEAT_RELEASE = 1.0


def extended(block, sides, width):
    for axis, dim in sides:
        count = lax.axis_size(axis)
        forward = [(i, i + 1) for i in range(count - 1)]
        forward.append((count - 1, 0))
        backward = [(target, source) for source, target in forward]
        low = lax.ppermute(
            lax.slice_in_dim(block, block.shape[dim] - width, None, axis=dim), axis, forward
        )
        high = lax.ppermute(lax.slice_in_dim(block, 0, width, axis=dim), axis, backward)
        block = jnp.concatenate([low, block, high], axis=dim)
    return block


def in_blocks(array, dim, peers):
    before, after = (array.shape[:dim], array.shape[dim + 1 :])
    return jnp.moveaxis(array.reshape(*before, peers, -1, *after), dim, 0)


def sum_at_owner(array, axis, dim):
    peers = lax.axis_size(axis)
    tiles = lax.all_to_all(in_blocks(array, dim, peers), axis, 0, 0, tiled=True)
    return jnp.sum(tiles, axis=0)


def copy_for_each(array, axis):
    copies = jnp.broadcast_to(array, (lax.axis_size(axis), *array.shape))
    return lax.all_to_all(copies, axis, split_axis=0, concat_axis=0, tiled=True)


def joined_along(tiles, dim):
    tiles = jnp.moveaxis(tiles, 0, dim)
    shape = tiles.shape
    return tiles.reshape(*shape[:dim], shape[dim] * shape[dim + 1], *shape[dim + 2 :])


def gather_directly(array, axis, dim):
    tiles = copy_for_each(array, axis)
    return joined_along(tiles, dim)


def inner_part(array, margin):
    return array[:, margin : array.shape[1] - margin, margin : array.shape[2] - margin]


def tendency(padded):
    n_x = padded.shape[1]
    n_y = padded.shape[2]
    pressure = 0.5 * padded[3]
    flux_x = padded[0][None] * padded
    flux_x = flux_x.at[0].add(pressure)
    flux_y = padded[1][None] * padded
    flux_y = flux_y.at[1].add(pressure)

    def along_x(shift):
        return (
            flux_x[:, 3 + shift : n_x - 3 + shift, 3 : n_y - 3]
            - flux_x[:, 3 - shift : n_x - 3 - shift, 3 : n_y - 3]
        )

    def along_y(shift):
        return (
            flux_y[:, 3 : n_x - 3, 3 + shift : n_y - 3 + shift]
            - flux_y[:, 3 : n_x - 3, 3 - shift : n_y - 3 - shift]
        )

    deriv_x = (45.0 * along_x(1) - 9.0 * along_x(2) + along_x(3)) / 60.0
    deriv_y = (45.0 * along_y(1) - 9.0 * along_y(2) + along_y(3)) / 60.0
    center = inner_part(padded, 3)
    react = REACT_RATE * center[2] * (1.0 + jnp.tanh(center[3]))
    zeros = jnp.zeros_like(react)
    source = jnp.stack([zeros, zeros, -react, HEAT_RELEASE * react])
    return source - deriv_x - deriv_y


def per_device(fields, factor_x, factor_y):
    high = lax.Precision.HIGHEST
    padded = extended(fields, (("gx", 1), ("gy", 2)), 9)
    section_one = inner_part(padded, 3) + TIME_STEP * tendency(padded)
    section_two = 0.75 * inner_part(padded, 6) + 0.25 * (
        inner_part(section_one, 3) + TIME_STEP * tendency(section_one)
    )
    advanced = 1.0 / 3.0 * inner_part(padded, 9) + 2.0 / 3.0 * (
        inner_part(section_two, 3) + TIME_STEP * tendency(section_two)
    )
    rank_full = factor_x.shape[1]
    count_x = lax.axis_size("gx")
    count_y = lax.axis_size("gy")
    partial_x = jnp.einsum("fxyz,xa->fayz", advanced, factor_x, precision=high)
    partial_value = sum_at_owner(partial_x, "gx", 1)
    local_core = jnp.einsum("fayz,yb->fabz", partial_value, factor_y, precision=high)
    core_tensor = sum_at_owner(local_core, "gy", 2)
    weights = factor_y
    columns = jnp.einsum(
        "fabz,yb->fayz", gather_directly(core_tensor, "gy", 2), weights, precision=high
    )
    weights = factor_x
    expanded = jnp.einsum(
        "fayz,xa->fxyz", gather_directly(columns, "gx", 1), weights, precision=high
    )
    total_x = factor_x.shape[0] * count_x
    total_y = factor_y.shape[0] * count_y
    rescale = math.sqrt(float(total_x) * float(total_y)) / rank_full
    rebuilt = rescale * expanded
    return (advanced, core_tensor, rebuilt)


def solution(mesh):
    placed = (P(None, "gx", "gy", None), P("gx", None), P("gy", None))
    return jax.shard_map(
        per_device,
        mesh=mesh,
        in_specs=placed,
        out_specs=(P(None, "gx", "gy", None), P(None, "gx", "gy", None), P(None, "gx", "gy", None)),
        check_vma=False,
    )
```

profile of v0, /device:TPU:1, one launch (start us, length us, event | category | flops | bytes accessed | tf_op | source)
XLA Modules:
  0.0 183.1 jit_solution(3243682545546000170)
XLA Ops:
  0.6 1.2 copy.8
  1.9 4.6 %collective-permute-start = (f32[4,9,16,128]{3,1,2,0:T(8,128)S(1)}, f32[4,9,16,128]{3,1,2,0:T(8,128)S(1)}, u32[]{:S(2)}, u32[]{:S(2)}) collective-permute-start(f32[4,9,16,128]{3,1,2,0:T(8,128)S(1)} %get-tuple-element.95), channel_id=1, source_target_pairs={{0,32},{32,64},{64,96},{96,128},{128,160},{160,192},{192,224},{224... | collective-permute-start | bytes 884744 | tf_op jit(solution)/shard_map/ppermute | solution.py:19
  6.5 13.4 %collective-permute-start.1 = (f32[4,9,16,128]{3,1,2,0:T(8,128)S(1)}, f32[4,9,16,128]{3,1,2,0:T(8,128)S(1)}, u32[]{:S(2)}, u32[]{:S(2)}) collective-permute-start(f32[4,9,16,128]{3,1,2,0:T(8,128)S(1)} %get-tuple-element.96), channel_id=1, source_target_pairs={{32,0},{64,32},{96,64},{128,96},{160,128},{192,160},{224,192},{256... | collective-permute-start | bytes 884744 | tf_op jit(solution)/shard_map/ppermute | solution.py:22
  19.9 1.5 collective-permute-done.1
  21.7 1.9 %collective-permute-start.2 = (f32[4,34,9,128]{3,1,2,0:T(8,128)S(1)}, f32[4,34,9,128]{3,1,2,0:T(8,128)S(1)}, u32[]{:S(2)}, u32[]{:S(2)}) collective-permute-start(f32[4,34,9,128]{3,1,2,0:T(8,128)S(1)} %get-tuple-element.91), channel_id=1, source_target_pairs={{0,1},{1,2},{2,3},{3,4},{4,5},{5,6},{6,7},{7,8},{8,9},{9,10},{10,1... | collective-permute-start | bytes 1880072 | tf_op jit(solution)/shard_map/ppermute | solution.py:19
  23.6 14.0 %collective-permute-start.3 = (f32[4,34,9,128]{3,1,2,0:T(8,128)S(1)}, f32[4,34,9,128]{3,1,2,0:T(8,128)S(1)}, u32[]{:S(2)}, u32[]{:S(2)}) collective-permute-start(f32[4,34,9,128]{3,1,2,0:T(8,128)S(1)} %get-tuple-element.92), channel_id=1, source_target_pairs={{1,0},{2,1},{3,2},{4,3},{5,4},{6,5},{7,6},{8,7},{9,8},{10,9},{11,1... | collective-permute-start | bytes 1880072 | tf_op jit(solution)/shard_map/ppermute | solution.py:22
  37.6 12.9 %collective-permute-done.2 = f32[4,34,9,128]{3,1,2,0:T(8,128)S(1)} collective-permute-done((f32[4,34,9,128]{3,1,2,0:T(8,128)S(1)}, f32[4,34,9,128]{3,1,2,0:T(8,128)S(1)}, u32[]{:S(2)}, u32[]{:S(2)}) %collective-permute-start.2) | collective-permute-done | bytes 626720 | tf_op jit(solution)/shard_map/ppermute | solution.py:19
  50.6 0.9 collective-permute-done.3
  51.9 0.3 broadcast_multiply_fusion.1
  52.9 3.1 %fusion.4 = f32[4,28,28,128]{3,1,2,0:T(8,128)S(1)} fusion(f32[4,34,34,128]{3,1,2,0:T(8,128)S(1)} %fusion.33, f32[4,34,34,128]{3,1,2,0:T(8,128)S(1)} %get-tuple-element.87, f32[4,34,34,128]{3,1,2,0:T(8,128)S(1)} %pad_maximum_fusion, f32[1,28,28,128]{3,1,2,0:T(8,128)S(1)} %get-tuple-element.86, f32[1,28,28,128]{3,1,2,0:T(8,128)S(1)} %get-tuple-element.85, ...), kind=kLoop, calls=%fused_computation.6 | loop fusion | flops 8830976 | bytes 23281680 | tf_op jit(solution)/shard_map/add | solution.py:91
  57.1 1.9 %fusion.21 = f32[4,22,22,128]{3,1,2,0:T(8,128)S(1)} fusion(f32[4,28,28,128]{3,1,2,0:T(8,128)S(1)} %fusion.51, f32[4,28,28,128]{3,1,2,0:T(8,128)S(1)} %get-tuple-element.89, f32[4,28,28,128]{3,1,2,0:T(8,128)S(1)} %fusion.4, f32[4,34,34,128]{3,1,2,0:T(8,128)S(1)} %pad_maximum_fusion, f32[1,22,22,128]{3,1,2,0:T(8,128)S(1)} %get-tuple-element.84, ...), kind=kLoop, calls=%fused_computation.36 | loop fusion | flops 6195200 | bytes 15364112 | tf_op jit(solution)/shard_map/add | solution.py:92
  59.4 0.9 copy-done.1
  60.3 0.8 fusion.41
  61.1 1.0 convolution_bitcast_fusion
  62.1 0.6 copy.12
  62.8 25.5 %all_to_all.20 = f32[32,4,1,16,128]{4,3,1,2,0:T(8,128)S(1)} all-to-all(f32[32,4,1,16,128]{4,3,1,2,0:T(8,128)S(1)} %copy.12), channel_id=1, replica_groups=mesh['gx'=32,'gy'=32] {'gx'}, dimensions={0} | all-to-all | bytes 2097152 | tf_op jit(solution)/shard_map/all_to_all | solution.py:34
  88.6 40.3 %all_to_all.21 = f32[32,4,1,1,128]{4,1,3,2,0:T(4,128)S(1)} all-to-all(f32[32,4,1,1,128]{4,1,3,2,0:T(4,128)S(1)} %copy.13), channel_id=1, replica_groups=mesh['gx'=32,'gy'=32] {'gy'}, dimensions={0} | all-to-all | bytes 131072 | tf_op jit(solution)/shard_map/all_to_all | solution.py:34
  129.0 26.5 %all_to_all.22 = f32[32,4,1,1,128]{4,1,3,2,0:T(4,128)S(1)} all-to-all(f32[32,4,1,1,128]{4,1,3,2,0:T(4,128)S(1)} %broadcast_in_dim.6), channel_id=1, replica_groups=mesh['gx'=32,'gy'=32] {'gy'}, dimensions={0} | all-to-all | bytes 131072 | tf_op jit(solution)/shard_map/all_to_all | solution.py:40
  155.7 1.1 broadcast_in_dim.7
  156.8 7.1 %all-to-all-start.3 = ((f32[32,4,1,16,128]{4,3,1,2,0:T(8,128)}), f32[32,4,1,16,128]{4,3,1,2,0:T(8,128)S(1)}, u32[]{:S(2)}, u32[]{:S(2)}) async-start(f32[32,4,1,16,128]{4,3,1,2,0:T(8,128)} %broadcast_in_dim.7), calls=%async_computation.3 | async-start | bytes 2097152 | tf_op jit(solution)/shard_map/all_to_all | solution.py:40
  163.9 1.0 copy.16
  164.8 16.0 %all-to-all-done.3 = f32[32,4,1,16,128]{4,3,1,2,0:T(8,128)S(1)} async-done(((f32[32,4,1,16,128]{4,3,1,2,0:T(8,128)}), f32[32,4,1,16,128]{4,3,1,2,0:T(8,128)S(1)}, u32[]{:S(2)}, u32[]{:S(2)}) %all-to-all-start.3) | async-done | bytes 1048608 | tf_op jit(solution)/shard_map/all_to_all | solution.py:40
  180.9 1.3 fusion.14
  182.1 1.0 copy.17
  (37 shorter events, 3.4 us)
Async XLA Ops:
  0.6 60.5 %copy-start = (f32[16,32]{1,0:T(8,128)S(1)}, f32[16,32]{1,0:T(8,128)}, u32[]{:S(2)}) copy-start(f32[16,32]{1,0:T(8,128)} %param.16) | copy-start | bytes 6148
  1.9 18.0 %collective-permute-start = (f32[4,9,16,128]{3,1,2,0:T(8,128)S(1)}, f32[4,9,16,128]{3,1,2,0:T(8,128)S(1)}, u32[]{:S(2)}, u32[]{:S(2)}) collective-permute-start(f32[4,9,16,128]{3,1,2,0:T(8,128)S(1)} %get-tuple-element.95), channel_id=1, source_target_pairs={{0,32},{32,64},{64,96},{96,128},{128,160},{160,192},{192,224},{224... | collective-permute-start | bytes 884744 | tf_op jit(solution)/shard_map/ppermute | solution.py:19
  6.5 14.9 %collective-permute-start.1 = (f32[4,9,16,128]{3,1,2,0:T(8,128)S(1)}, f32[4,9,16,128]{3,1,2,0:T(8,128)S(1)}, u32[]{:S(2)}, u32[]{:S(2)}) collective-permute-start(f32[4,9,16,128]{3,1,2,0:T(8,128)S(1)} %get-tuple-element.96), channel_id=1, source_target_pairs={{32,0},{64,32},{96,64},{128,96},{160,128},{192,160},{224,192},{256... | collective-permute-start | bytes 884744 | tf_op jit(solution)/shard_map/ppermute | solution.py:22
  21.7 28.9 %collective-permute-start.2 = (f32[4,34,9,128]{3,1,2,0:T(8,128)S(1)}, f32[4,34,9,128]{3,1,2,0:T(8,128)S(1)}, u32[]{:S(2)}, u32[]{:S(2)}) collective-permute-start(f32[4,34,9,128]{3,1,2,0:T(8,128)S(1)} %get-tuple-element.91), channel_id=1, source_target_pairs={{0,1},{1,2},{2,3},{3,4},{4,5},{5,6},{6,7},{7,8},{8,9},{9,10},{10,1... | collective-permute-start | bytes 1880072 | tf_op jit(solution)/shard_map/ppermute | solution.py:19
  23.6 27.9 %collective-permute-start.3 = (f32[4,34,9,128]{3,1,2,0:T(8,128)S(1)}, f32[4,34,9,128]{3,1,2,0:T(8,128)S(1)}, u32[]{:S(2)}, u32[]{:S(2)}) collective-permute-start(f32[4,34,9,128]{3,1,2,0:T(8,128)S(1)} %get-tuple-element.92), channel_id=1, source_target_pairs={{1,0},{2,1},{3,2},{4,3},{5,4},{6,5},{7,6},{8,7},{9,8},{10,9},{11,1... | collective-permute-start | bytes 1880072 | tf_op jit(solution)/shard_map/ppermute | solution.py:22
  59.2 1.0 copy-start.1
  62.7 25.6 %copy-start.2 = (f32[16,32]{1,0:T(8,128)S(1)}, f32[16,32]{1,0:T(8,128)}, u32[]{:S(2)}) copy-start(f32[16,32]{1,0:T(8,128)} %param.17) | copy-start | bytes 6148
  129.0 35.9 %copy-start.3 = (f32[4,128]{1,0:T(4,128)}, f32[4,128]{1,0:T(4,128)S(1)}, u32[]{:S(2)}) copy-start(f32[4,128]{1,0:T(4,128)S(1)} %reduce_sum.21) | copy-start | bytes 6148
  156.8 24.1 %all-to-all-start.3 = ((f32[32,4,1,16,128]{4,3,1,2,0:T(8,128)}), f32[32,4,1,16,128]{4,3,1,2,0:T(8,128)S(1)}, u32[]{:S(2)}, u32[]{:S(2)}) async-start(f32[32,4,1,16,128]{4,3,1,2,0:T(8,128)} %broadcast_in_dim.7), calls=%async_computation.3 | async-start | bytes 2097152 | tf_op jit(solution)/shard_map/all_to_all | solution.py:40
where the time goes:
time: 184 us; the launch traced here: 183 us
  blocking collectives  92.3 us (50%)
  starting transfers between devices  41 us (22%)
  waiting for transfers between devices  31.4 us (17%)
  other arithmetic  8.74 us (5%)
  local copies, waits for them, and re-layouts  6.05 us (3%)
  matrix products  2.71 us (1%)
    all_to_all x2, blocking collectives, sum_at_owner(): tiles = lax.all_to_all(in_blocks(array, dim, peers), axis, 0, 0, tiled=True)  65.8 us
    ppermute x2, starting transfers between devices, extended(): lax.ppermute(lax.slice_in_dim(block, 0, width, axis=dim), axis, backward)  27.4 us
    all_to_all x1, blocking collectives, copy_for_each(): return lax.all_to_all(copies, axis, split_axis=0, concat_axis=0, tiled=True)  26.5 us
    all_to_all x1, waiting for transfers between devices, copy_for_each(): return lax.all_to_all(copies, axis, split_axis=0, concat_axis=0, tiled=True)  16 us
    ppermute x2, waiting for transfers between devices, extended(): lax.ppermute(lax.slice_in_dim(block, block.shape[dim] - width, None, axis...  12.9 us
    all_to_all x1, starting transfers between devices, copy_for_each(): return lax.all_to_all(copies, axis, split_axis=0, concat_axis=0, tiled=True)  7.08 us
    ppermute x2, starting transfers between devices, extended(): lax.ppermute(lax.slice_in_dim(block, block.shape[dim] - width, None, axis...  6.5 us
    unnamed x11, local copies, waits for them, and re-layouts  4.02 us
  transfers between devices with their start and end apart: 5, of which 4 were waited for; matrix products, arithmetic and copies ran while one was open for 1% of the time, Pallas kernels for 0%

commit v1 on v0

v1 whole, which is shorter than its diff:
```python
import functools
import math

import jax
import jax.numpy as jnp
from jax import lax
from jax.experimental import pallas as pl
from jax.experimental.pallas import tpu as pltpu
from jax.sharding import PartitionSpec as P

TIME_STEP = 0.2
REACT_RATE = 0.5
HEAT_RELEASE = 1.0
HIGH = lax.Precision.HIGHEST
SECTIONS = ((0.0, 1.0), (0.75, 0.25), (1.0 / 3.0, 2.0 / 3.0))
LOW, TOP = 0, 1
N = 16
F = 4
W = 3
RANK = 32
CHIPS = 16
CHUNKS = 2
FC = F // CHUNKS


def far_first(count):
    order = []
    for k in range(count // 2, 0, -1):
        order += [k] if 2 * k == count else [k, count - k]
    return order


Z_ORDER = far_first(32)


def in_plane_order():
    def hops(k):
        y, x = k % 4, k // 4
        return min(y, 4 - y) + min(x, 4 - x)

    return sorted(range(1, CHIPS), key=lambda k: -hops(k))


PLANE_ORDER = in_plane_order()


def iota(shape, dim):
    return lax.broadcasted_iota(jnp.int32, shape, dim)


def dot(a, b, contract=((1,), (0,))):
    return lax.dot_general(
        a, b, (contract, ((), ())), precision=HIGH, preferred_element_type=jnp.float32
    )


def one_hot(hit):
    return jnp.where(hit, 1.0, 0.0).astype(jnp.float32)


def spread(rows, cells):
    n, k = rows.shape
    wide = dot(rows, one_hot(iota((k, 8 * k), 1) // 8 == iota((k, 8 * k), 0)))
    same = iota((n, 8 * k), 0) % 8 == iota((n, 8 * k), 1) % 8
    return jnp.where(same, wide, 0.0)


def kernel(
    rescale,
    fields, fx, fy,
    adv, core_out, reb,
    state, flux_x, flux_y, halo_x, halo_y, edge_y,
    mate_adv, fx_own, fx_mate, part, part_in, local, core_in, core_own, core_all, cols, gathered,
    lhs_in, lhs_out, fy_t,
    load_sem, halo_send, halo_recv, fx_sems, mate_send, mate_recv,
    plane_send, plane_recv, z_send, z_recv, zb_send, zb_recv, back_send, back_recv, pass_send, pass_recv,
    near_sem,
):
    gx, gy = lax.axis_index("gx"), lax.axis_index("gy")
    core = lax.rem(gx, 2)
    mate = {"gx": gx + 1 - 2 * core}

    def along(axis, offset):
        count, me = 32, (gx if axis == "gx" else gy)
        return {axis: lax.rem(me + (offset + count), count)}

    def signal(sem, target):
        pl.semaphore_signal(sem, inc=1, device_id=target, device_id_type=pl.DeviceIdType.MESH)

    def copy(src, dst, send, recv, target):
        return pltpu.make_async_remote_copy(
            src_ref=src, dst_ref=dst, send_sem=send, recv_sem=recv,
            device_id=target, device_id_type=pl.DeviceIdType.MESH,
        )

    def take_all(sem, ref):
        pltpu.make_async_copy(ref, ref, sem).wait()

    load = pltpu.make_async_copy(fields, state.at[0], load_sem)
    load.start()
    barrier = pltpu.get_barrier_semaphore()
    for axis in ("gx", "gy"):
        for side in (-1, 1):
            signal(barrier, along(axis, side))

    fx_own[...] = jnp.zeros_like(fx_own)
    fx_own[:, 0:RANK] = fx[...]
    zero_rows = jnp.zeros((8, 128), jnp.float32)

    @pl.loop(0, N)
    def _(x):
        for f in range(F):
            flux_y[f, x, 0:8, :] = zero_rows
            flux_y[f, x, 24:32, :] = zero_rows

    pl.semaphore_wait(barrier, 4)

    def sign_in(level):
        for i, axis in enumerate(("gx", "gy")):
            for side in (-1, 1):
                signal(near_sem.at[i, level], along(axis, side * (1 << level)))

    def signed_in(level):
        for i in range(2):
            pl.semaphore_wait(near_sem.at[i, level], 2)

    sign_in(0)
    fx_copy = copy(fx_own, fx_mate, fx_sems.at[0], fx_sems.at[1], mate)
    fx_copy.start()
    load.wait()

    def flat(s):
        return (adv if s == 3 else state.at[s]).reshape(F * N * N, 128)

    for f in range(F):
        for j in range(W):
            edge_y[0, LOW, f, j] = flat(0)[pl.ds(f * N * N + j, N, stride=N), :]
            edge_y[0, TOP, f, j] = flat(0)[pl.ds(f * N * N + N - W + j, N, stride=N), :]

    def halo_copies(s):
        now = state.at[s]
        return (
            copy(edge_y.at[s, LOW], halo_y.at[s, TOP], halo_send.at[s, 0], halo_recv.at[s, 0], along("gy", -1)),
            copy(edge_y.at[s, TOP], halo_y.at[s, LOW], halo_send.at[s, 1], halo_recv.at[s, 1], along("gy", 1)),
            copy(now.at[:, pl.ds(0, W)], halo_x.at[s, TOP], halo_send.at[s, 2], halo_recv.at[s, 2], along("gx", -1)),
            copy(now.at[:, pl.ds(N - W, W)], halo_x.at[s, LOW], halo_send.at[s, 3], halo_recv.at[s, 3], along("gx", 1)),
        )

    def fluxes(values, which):
        total = [values[which] * v for v in values]
        total[which] = total[which] + 0.5 * values[3]
        return total

    def section(s):
        keep, take = SECTIONS[s]
        now, base = state.at[s], state.at[0]
        after = adv if s == 2 else state.at[s + 1]
        copies = halo_copies(s)
        for c in copies:
            c.start()

        @pl.loop(0, N)
        def _(x):
            for t in range(2):
                rows = pl.ds(8 * t, 8)
                values = [now[f, x, rows, :] for f in range(F)]
                for f, g in enumerate(fluxes(values, 0)):
                    flux_x[f, x + W, rows, :] = g
                for f, g in enumerate(fluxes(values, 1)):
                    flux_y[f, x, pl.ds(8 + 8 * t, 8), :] = g

        scale = take * TIME_STEP / 60.0

        def advance(x):
            for t in range(2):
                rows = pl.ds(8 * t, 8)
                heat = now[3, x, rows, :]
                react = (take * TIME_STEP * REACT_RATE) * now[2, x, rows, :] * (1.0 + jnp.tanh(heat))
                for f in range(F):
                    def pair(shift):
                        in_x = flux_x[f, x + (W + shift), rows, :] - flux_x[f, x + (W - shift), rows, :]
                        start = 8 + 8 * t
                        in_y = flux_y[f, x, pl.ds(start + shift, 8), :] - flux_y[f, x, pl.ds(start - shift, 8), :]
                        return in_x + in_y

                    slope = (45.0 * scale) * pair(1) - (9.0 * scale) * pair(2) + scale * pair(3)
                    new = take * now[f, x, rows, :] - slope
                    if keep:
                        new = new + keep * base[f, x, rows, :]
                    if f == 2:
                        new = new - react
                    if f == 3:
                        new = new + HEAT_RELEASE * react
                    after[f, x, rows, :] = new

        @pl.loop(W, N - W)
        def _(x):
            advance(x)

        if s < 2:
            signed_in(s)
            sign_in(s + 1)
        copies[2].wait_recv()
        copies[3].wait_recv()
        for side, first in ((LOW, 0), (TOP, N + W)):
            @pl.loop(0, W)
            def _(j):
                for t in range(2):
                    rows = pl.ds(8 * t, 8)
                    values = [halo_x[s, side, f, j, rows, :] for f in range(F)]
                    for f, g in enumerate(fluxes(values, 0)):
                        flux_x[f, first + j, rows, :] = g

        @pl.loop(0, W)
        def _(j):
            advance(j)
            advance(N - W + j)

        if s == 1:
            signed_in(2)
            sign_in(3)
        copies[0].wait_recv()
        copies[1].wait_recv()
        out = flat(s + 1)
        for side in (LOW, TOP):
            sign = 1.0 if side == LOW else -1.0
            near = (2, 1, 0) if side == LOW else (0, 1, 2)
            flux = []
            for j in near:
                flux.append(fluxes([halo_y[s, side, f, j] for f in range(F)], 1))
            for f in range(F):
                g1, g2, g3 = (flux[k][f] for k in range(W))
                changes = (
                    (sign * 45.0 * scale) * g1 - (sign * 9.0 * scale) * g2 + (sign * scale) * g3,
                    (sign * scale) * g2 - (sign * 9.0 * scale) * g1,
                    (sign * scale) * g1,
                )
                for k, change in enumerate(changes):
                    y = k if side == LOW else N - 1 - k
                    at = pl.ds(f * N * N + y, N, stride=N)
                    new = out[at, :] + change
                    out[at, :] = new
                    if s < 2:
                        edge_y[s + 1, side, f, k if side == LOW else W - 1 - k] = new
        return copies

    sent = []
    sent += section(0)
    fx_copy.wait_recv()
    picked = one_hot(iota((128, RANK), 1) == 2 * (iota((128, RANK), 0) // 8) + core)
    for half, factor in ((0, fx_own), (1, fx_mate)):
        rows = dot(picked, factor[:, 0:RANK], ((1,), (1,)))
        lhs_in[:, 128 * half : 128 * half + 128] = spread(rows, N)
    rows = dot(one_hot(iota((128, N), 0) // 8 == iota((128, N), 1)), fx_own[:, 0:RANK])
    lhs_out[...] = rescale * spread(rows, RANK)
    fy_t[...] = dot(one_hot(iota((RANK, RANK), 0) == iota((RANK, RANK), 1)), fy[...], ((1,), (1,)))
    sent += section(1)
    sent += section(2)

    mates = []
    for c in range(CHUNKS):
        piece = pl.ds(c * FC, FC)
        mates.append(copy(adv.at[piece], mate_adv.at[piece], mate_send.at[c], mate_recv.at[c], mate))
        mates[-1].start()
    signed_in(3)
    sent += mates

    def tiles(ref, f):
        return jnp.concatenate(
            [ref[f, :, 8 * t : 8 * t + 8, :].reshape(8 * N, 128) for t in range(2)], axis=1
        )

    chip = gx // 2
    plane = []
    for c in range(CHUNKS):
        mates[c].wait_recv()
        for i in range(FC):
            f = c * FC + i
            both = jnp.concatenate([tiles(adv, f), tiles(mate_adv, f)], axis=0)
            total = dot(lhs_in[...], both)
            for t in range(2):
                part[c, :, i, 8 * t : 8 * t + 8, :] = total[:, 128 * t : 128 * t + 128].reshape(CHIPS, 8, 128)
        for k in PLANE_ORDER:
            to = lax.rem(chip + k, CHIPS)
            plane.append(
                copy(part.at[c, to], part_in.at[c, k - 1], plane_send.at[c], plane_recv.at[c], {"gx": 2 * to + core})
            )
            plane[-1].start()

    out_z = []
    for c in range(CHUNKS):
        take_all(plane_recv.at[c], part_in.at[c])
        for i in range(FC):
            total = part[c, chip, i]
            for k in range(CHIPS - 1):
                total = total + part_in[c, k, i]
            local[c, :, i, :] = dot(fy_t[...], total)
        for k in Z_ORDER:
            to = lax.rem(gy + k, 32)
            out_z.append(copy(local.at[c, to], core_in.at[c, k - 1], z_send.at[c], z_recv.at[c], {"gy": to}))
            out_z[-1].start()

    back_z = []
    for c in range(CHUNKS):
        take_all(z_recv.at[c], core_in.at[c])
        total = local[c, gy]
        for k in range(31):
            total = total + core_in[c, k]
        core_own[c] = total
        core_all[c, gy] = total
        core_out[c * FC : c * FC + FC, :] = total
        for k in Z_ORDER:
            to = lax.rem(gy + k, 32)
            back_z.append(copy(core_own.at[c], core_all.at[c, gy], zb_send.at[c], zb_recv.at[c], {"gy": to}))
            back_z[-1].start()

    back = []
    passed = []
    for c in range(CHUNKS):
        take_all(zb_recv.at[c], core_all.at[c, pl.ds(0, 31)])
        for i in range(FC):
            expanded = dot(fy[...], core_all[c, :, i, :])
            cols[c, i] = expanded
            gathered[c, gx, i] = expanded
        for k in PLANE_ORDER:
            to = lax.rem(chip + k, CHIPS)
            back.append(
                copy(cols.at[c], gathered.at[c, gx], back_send.at[c], back_recv.at[c, k - 1], {"gx": 2 * to + core})
            )
            back[-1].start()
        passed.append(copy(cols.at[c], gathered.at[c, gx], pass_send.at[c], pass_recv.at[c], mate))
        passed[-1].start()
    for c in range(CHUNKS):
        for n, k in reversed(list(enumerate(PLANE_ORDER))):
            back[c * (CHIPS - 1) + n].wait_recv()
            came = 2 * lax.rem(chip + (CHIPS - k), CHIPS) + core
            passed.append(
                copy(gathered.at[c, came], gathered.at[c, came], pass_send.at[c], pass_recv.at[c], mate)
            )
            passed[-1].start()
    for c in range(CHUNKS):
        take_all(pass_recv.at[c], gathered.at[c, pl.ds(0, CHIPS)])
        for i in range(FC):
            both = jnp.concatenate(
                [gathered[c, :, i, 8 * t : 8 * t + 8, :].reshape(8 * RANK, 128) for t in range(2)], axis=1
            )
            whole = dot(lhs_out[...], both)
            for t in range(2):
                reb[c * FC + i, :, 8 * t : 8 * t + 8, :] = whole[:, 128 * t : 128 * t + 128].reshape(N, 8, 128)

    for c in sent + [fx_copy]:
        c.wait_send()
    for c in range(CHUNKS):
        take_all(plane_send.at[c], part_in.at[c])
        take_all(z_send.at[c], core_in.at[c])
        take_all(zb_send.at[c], core_all.at[c, pl.ds(0, 31)])
        take_all(back_send.at[c], gathered.at[c, pl.ds(0, CHIPS - 1)])
        take_all(pass_send.at[c], gathered.at[c, pl.ds(0, CHIPS)])


def per_device(fields, factor_x, factor_y):
    total_x, total_y = factor_x.shape[0] * 32, factor_y.shape[0] * 32
    rescale = math.sqrt(float(total_x) * float(total_y)) / factor_x.shape[1]
    f32 = jnp.float32
    vmem = pltpu.VMEM
    dma = pltpu.SemaphoreType.DMA
    whole = (F, N, N, 128)
    scratch = [
        vmem((3, *whole), f32),
        vmem((F, N + 2 * W, N, 128), f32),
        vmem((F, N, 2 * N, 128), f32),
        vmem((3, 2, F, W, N, 128), f32),
        vmem((3, 2, F, W, N, 128), f32),
        vmem((3, 2, F, W, N, 128), f32),
        vmem(whole, f32),
        vmem((N, 128), f32),
        vmem((N, 128), f32),
        vmem((CHUNKS, CHIPS, FC, N, 128), f32),
        vmem((CHUNKS, CHIPS - 1, FC, N, 128), f32),
        vmem((CHUNKS, RANK, FC, 128), f32),
        vmem((CHUNKS, 31, FC, 128), f32),
        vmem((CHUNKS, FC, 128), f32),
        vmem((CHUNKS, RANK, FC, 128), f32),
        vmem((CHUNKS, FC, N, 128), f32),
        vmem((CHUNKS, RANK, FC, N, 128), f32),
        vmem((128, 256), f32),
        vmem((128, 256), f32),
        vmem((RANK, N), f32),
        dma,
        dma((3, 4)), dma((3, 4)), dma((2,)), dma((CHUNKS,)), dma((CHUNKS,)),
        dma((CHUNKS,)), dma((CHUNKS,)), dma((CHUNKS,)), dma((CHUNKS,)),
        dma((CHUNKS,)), dma((CHUNKS,)),
        dma((CHUNKS,)), dma((CHUNKS, CHIPS - 1)), dma((CHUNKS,)), dma((CHUNKS,)),
        pltpu.SemaphoreType.REGULAR((2, 4)),
    ]
    advanced, core, rebuilt = pl.pallas_call(
        functools.partial(kernel, rescale),
        out_shape=(
            jax.ShapeDtypeStruct(whole, f32),
            jax.ShapeDtypeStruct((F, 128), f32),
            jax.ShapeDtypeStruct(whole, f32),
        ),
        in_specs=[
            pl.BlockSpec(memory_space=pl.ANY),
            pl.BlockSpec(memory_space=pltpu.VMEM),
            pl.BlockSpec(memory_space=pltpu.VMEM),
        ],
        out_specs=[pl.BlockSpec(memory_space=pltpu.VMEM)] * 3,
        scratch_shapes=scratch,
        compiler_params=pltpu.CompilerParams(collective_id=0, has_side_effects=True),
        name="flow_tucker",
    )(fields, factor_x, factor_y)
    return advanced, core.reshape(F, 1, 1, 128), rebuilt


def solution(mesh):
    placed = P(None, "gx", "gy", None)
    return jax.shard_map(
        per_device,
        mesh=mesh,
        in_specs=(placed, P("gx", None), P("gy", None)),
        out_specs=(placed, placed, placed),
        check_vma=False,
    )
```

time: 184 us -> 85 us (0.46)
  blocking collectives: 92.3 us -> 0 us
  Pallas kernels: 0 us -> 80.8 us
  starting transfers between devices: 41 us -> 0 us
  waiting for transfers between devices: 31.4 us -> 0 us
  other arithmetic: 8.74 us -> 0 us
  local copies, waits for them, and re-layouts: 6.05 us -> 3.31 us
  matrix products: 2.71 us -> 0 us
    all_to_all x3 -> x0, blocking collectives: 92.3 us -> none  [the longest x2 65.8 us: sum_at_owner(): tiles = lax.all_to_all(in_blocks(array, dim, peers), axis, 0, 0, tiled=True)]
    pallas_call x0 -> x1, Pallas kernels: none -> 80.8 us  [per_device(): pl.pallas_call(functools.partial(kernel, rescale), out_shape=(jax.ShapeDt...]
    ppermute x4 -> x0, starting transfers between devices: 33.9 us -> none  [the longest x2 27.4 us: extended(): lax.ppermute(lax.slice_in_dim(block, 0, width, axis=dim), axis, backward)]
    all_to_all x1 -> x0, waiting for transfers between devices: 16 us -> none  [copy_for_each(): return lax.all_to_all(copies, axis, split_axis=0, concat_axis=0, tiled=True)]
    ppermute x4 -> x0, waiting for transfers between devices: 15.3 us -> none  [the longest x2 12.9 us: extended(): lax.ppermute(lax.slice_in_dim(block, block.shape[dim] - width, None, axis...]
    all_to_all x1 -> x0, starting transfers between devices: 7.08 us -> none  [copy_for_each(): return lax.all_to_all(copies, axis, split_axis=0, concat_axis=0, tiled=True)]
    add x3 -> x0, other arithmetic: 5.8 us -> none  [the longest x1 3.12 us: per_device(): section_one = inner_part(padded, 3) + TIME_STEP * tendency(padded)]
    dot_general x4 -> x0, matrix products: 2.71 us -> none  [the longest x1 1.27 us: per_device(): jnp.einsum('fayz,xa->fxyz', gather_directly(columns, 'gx', 1), weights, p...]
  transfers between devices with their start and end apart: 5 -> 0, of which waited for: 4 -> 0; matrix products, arithmetic and copies ran while one was open for 1% -> 0% of each run, Pallas kernels for 0% -> 0%
where the time goes in v1:
time: 85 us; the launch traced here: 84.8 us
  Pallas kernels  80.8 us (95%)
  local copies, waits for them, and re-layouts  3.31 us (4%)
    pallas_call x1, Pallas kernels, per_device(): pl.pallas_call(functools.partial(kernel, rescale), out_shape=(jax.ShapeDt...  80.8 us
    unnamed x7, local copies, waits for them, and re-layouts  3.31 us

profile of v1, /device:TPU:1, one launch (start us, length us, event | category | flops | bytes accessed | tf_op | source)
XLA Modules:
  0.0 84.8 jit_solution(18198993574688143331)
XLA Ops:
  0.6 80.8 %flow_tucker.1 = (f32[4,16,16,128]{3,2,1,0:T(8,128)}, f32[4,128]{1,0:T(4,128)}, f32[4,16,16,128]{3,2,1,0:T(8,128)}) custom-call(f32[4,16,16,128]{3,2,1,0:T(8,128)} %fields.1, f32[16,32]{1,0:T(8,128)} %fx.1, f32[16,32]{1,0:T(8,128)} %fy.1), custom_call_target="tpu_custom_call" | custom-call | tf_op jit(solution)/shard_map/flow_tucker/pallas_call | solution.py:396
  81.4 0.0 copy-start.1
  81.4 0.0 copy-start
  81.5 1.9 %copy.10 = f32[4,16,16,128]{3,2,1,0:T(8,128)} copy(f32[4,16,16,128]{3,2,1,0:T(8,128)} %get-tuple-element.15) | data formatting | bytes 1048576
  83.4 0.0 copy-done.1
  83.4 0.6 copy.11
  84.0 0.0 copy-done
  84.0 0.8 copy.12
Async XLA Ops:
  81.4 1.9 %copy-start.1 = (f32[4,128]{1,0:T(4,128)S(1)}, f32[4,128]{1,0:T(4,128)}, u32[]{:S(2)}) copy-start(f32[4,128]{1,0:T(4,128)} %get-tuple-element.7) | copy-start | bytes 6148
  81.4 2.5 %copy-start = (f32[4,16,16,128]{3,2,1,0:T(8,128)S(1)}, f32[4,16,16,128]{3,2,1,0:T(8,128)}, u32[]{:S(2)}) copy-start(f32[4,16,16,128]{3,2,1,0:T(8,128)} %get-tuple-element.17) | copy-start | bytes 1572868

commit v2 on v1

--- a/solution.py
+++ b/solution.py
@@ -16,6 +16,7 @@
 LOW, TOP = 0, 1
 N = 16
 F = 4
+VMEM_BYTES = 65500000
 W = 3
 RANK = 32
 CHIPS = 16
@@ -65,14 +66,24 @@
     return jnp.where(same, wide, 0.0)
 
 
+def expand(lhs, columns, write):
+    for i in range(FC):
+        both = jnp.concatenate(
+            [columns[:, i, 8 * t : 8 * t + 8, :].reshape(8 * RANK, 128) for t in range(2)], axis=1
+        )
+        whole = dot(lhs[...], both)
+        for t in range(2):
+            write(i, t, whole[:, 128 * t : 128 * t + 128].reshape(N, 8, 128))
+
+
 def kernel(
     rescale,
-    fields, fx, fy,
-    adv, core_out, reb,
+    fields, fx_in, fy_in,
+    adv, core_out, reb, last, lhs_out,
     state, flux_x, flux_y, halo_x, halo_y, edge_y,
-    mate_adv, fx_own, fx_mate, part, part_in, local, core_in, core_own, core_all, cols, gathered,
-    lhs_in, lhs_out, fy_t,
-    load_sem, halo_send, halo_recv, fx_sems, mate_send, mate_recv,
+    mate_adv, fx_own, fx_mate, part, part_in, local, core_in, core_own, core_all, cols, ahead,
+    lhs_in, fy_t, fy,
+    load_sem, factor_sems, halo_send, halo_recv, fx_sems, mate_send, mate_recv,
     plane_send, plane_recv, z_send, z_recv, zb_send, zb_recv, back_send, back_recv, pass_send, pass_recv,
     near_sem,
 ):
@@ -98,13 +109,17 @@
 
     load = pltpu.make_async_copy(fields, state.at[0], load_sem)
     load.start()
+    factors = [
+        pltpu.make_async_copy(fx_in, fx_own, factor_sems.at[0]),
+        pltpu.make_async_copy(fy_in, fy, factor_sems.at[1]),
+    ]
+    for c in factors:
+        c.start()
     barrier = pltpu.get_barrier_semaphore()
     for axis in ("gx", "gy"):
         for side in (-1, 1):
             signal(barrier, along(axis, side))
 
-    fx_own[...] = jnp.zeros_like(fx_own)
-    fx_own[:, 0:RANK] = fx[...]
     zero_rows = jnp.zeros((8, 128), jnp.float32)
 
     @pl.loop(0, N)
@@ -126,6 +141,8 @@
 
     sign_in(0)
     fx_copy = copy(fx_own, fx_mate, fx_sems.at[0], fx_sems.at[1], mate)
+    for c in factors:
+        c.wait()
     fx_copy.start()
     load.wait()
 
@@ -150,6 +167,16 @@
         total = [values[which] * v for v in values]
         total[which] = total[which] + 0.5 * values[3]
         return total
+
+    def prepare():
+        fx_copy.wait_recv()
+        picked = one_hot(iota((128, RANK), 1) == 2 * (iota((128, RANK), 0) // 8) + core)
+        for half, factor in ((0, fx_own), (1, fx_mate)):
+            rows = dot(picked, factor[...], ((1,), (1,)))
+            lhs_in[:, 128 * half : 128 * half + 128] = spread(rows, N)
+        rows = dot(one_hot(iota((128, N), 0) // 8 == iota((128, N), 1)), fx_own[...])
+        lhs_out[...] = rescale * spread(rows, RANK)
+        fy_t[...] = dot(one_hot(iota((RANK, RANK), 0) == iota((RANK, RANK), 1)), fy[...], ((1,), (1,)))
 
     def section(s):
         keep, take = SECTIONS[s]
@@ -200,6 +227,8 @@
         if s < 2:
             signed_in(s)
             sign_in(s + 1)
+        if s == 1:
+            prepare()
         copies[2].wait_recv()
         copies[3].wait_recv()
         for side, first in ((LOW, 0), (TOP, N + W)):
@@ -222,14 +251,13 @@
         copies[0].wait_recv()
         copies[1].wait_recv()
         out = flat(s + 1)
-        for side in (LOW, TOP):
-            sign = 1.0 if side == LOW else -1.0
-            near = (2, 1, 0) if side == LOW else (0, 1, 2)
-            flux = []
-            for j in near:
-                flux.append(fluxes([halo_y[s, side, f, j] for f in range(F)], 1))
-            for f in range(F):
-                g1, g2, g3 = (flux[k][f] for k in range(W))
+        flux = []
+        for side, near in ((LOW, (2, 1, 0)), (TOP, (0, 1, 2))):
+            flux.append([fluxes([halo_y[s, side, f, j] for f in range(F)], 1) for j in near])
+        for f in range(F):
+            for side in (LOW, TOP):
+                sign = 1.0 if side == LOW else -1.0
+                g1, g2, g3 = (flux[side][k][f] for k in range(W))
                 changes = (
                     (sign * 45.0 * scale) * g1 - (sign * 9.0 * scale) * g2 + (sign * scale) * g3,
                     (sign * scale) * g2 - (sign * 9.0 * scale) * g1,
@@ -242,26 +270,19 @@
                     out[at, :] = new
                     if s < 2:
                         edge_y[s + 1, side, f, k if side == LOW else W - 1 - k] = new
+            if s == 2 and (f + 1) % FC == 0:
+                c = f // FC
+                piece = pl.ds(c * FC, FC)
+                mates.append(copy(adv.at[piece], mate_adv.at[piece], mate_send.at[c], mate_recv.at[c], mate))
+                mates[-1].start()
         return copies
 
+    mates = []
     sent = []
     sent += section(0)
-    fx_copy.wait_recv()
-    picked = one_hot(iota((128, RANK), 1) == 2 * (iota((128, RANK), 0) // 8) + core)
-    for half, factor in ((0, fx_own), (1, fx_mate)):
-        rows = dot(picked, factor[:, 0:RANK], ((1,), (1,)))
-        lhs_in[:, 128 * half : 128 * half + 128] = spread(rows, N)
-    rows = dot(one_hot(iota((128, N), 0) // 8 == iota((128, N), 1)), fx_own[:, 0:RANK])
-    lhs_out[...] = rescale * spread(rows, RANK)
-    fy_t[...] = dot(one_hot(iota((RANK, RANK), 0) == iota((RANK, RANK), 1)), fy[...], ((1,), (1,)))
     sent += section(1)
     sent += section(2)
 
-    mates = []
-    for c in range(CHUNKS):
-        piece = pl.ds(c * FC, FC)
-        mates.append(copy(adv.at[piece], mate_adv.at[piece], mate_send.at[c], mate_recv.at[c], mate))
-        mates[-1].start()
     signed_in(3)
     sent += mates
 
@@ -308,7 +329,7 @@
             total = total + core_in[c, k]
         core_own[c] = total
         core_all[c, gy] = total
-        core_out[c * FC : c * FC + FC, :] = total
+        core_out[c * FC : c * FC + FC] = total.reshape(FC, 1, 1, 128)
         for k in Z_ORDER:
             to = lax.rem(gy + k, 32)
             back_z.append(copy(core_own.at[c], core_all.at[c, gy], zb_send.at[c], zb_recv.at[c], {"gy": to}))
@@ -316,37 +337,40 @@
 
     back = []
     passed = []
+    gathered = [ahead.at[c] for c in range(CHUNKS - 1)] + [last]
     for c in range(CHUNKS):
         take_all(zb_recv.at[c], core_all.at[c, pl.ds(0, 31)])
         for i in range(FC):
             expanded = dot(fy[...], core_all[c, :, i, :])
             cols[c, i] = expanded
-            gathered[c, gx, i] = expanded
+            gathered[c][gx, i] = expanded
         for k in PLANE_ORDER:
             to = lax.rem(chip + k, CHIPS)
             back.append(
-                copy(cols.at[c], gathered.at[c, gx], back_send.at[c], back_recv.at[c, k - 1], {"gx": 2 * to + core})
+                copy(cols.at[c], gathered[c].at[gx], back_send.at[c], back_recv.at[c, k - 1], {"gx": 2 * to + core})
             )
             back[-1].start()
-        passed.append(copy(cols.at[c], gathered.at[c, gx], pass_send.at[c], pass_recv.at[c], mate))
+        passed.append(copy(cols.at[c], gathered[c].at[gx], pass_send.at[c], pass_recv.at[c], mate))
         passed[-1].start()
+    def settle(c):
+        take_all(pass_recv.at[c], gathered[c].at[pl.ds(0, CHIPS)])
+
+        def write(i, t, values):
+            reb[c * FC + i, :, 8 * t : 8 * t + 8, :] = values
+
+        expand(lhs_out, gathered[c], write)
+
     for c in range(CHUNKS):
         for n, k in reversed(list(enumerate(PLANE_ORDER))):
             back[c * (CHIPS - 1) + n].wait_recv()
             came = 2 * lax.rem(chip + (CHIPS - k), CHIPS) + core
             passed.append(
-                copy(gathered.at[c, came], gathered.at[c, came], pass_send.at[c], pass_recv.at[c], mate)
+                copy(gathered[c].at[came], gathered[c].at[came], pass_send.at[c], pass_recv.at[c], mate)
             )
             passed[-1].start()
-    for c in range(CHUNKS):
-        take_all(pass_recv.at[c], gathered.at[c, pl.ds(0, CHIPS)])
-        for i in range(FC):
-            both = jnp.concatenate(
-                [gathered[c, :, i, 8 * t : 8 * t + 8, :].reshape(8 * RANK, 128) for t in range(2)], axis=1
-            )
-            whole = dot(lhs_out[...], both)
-            for t in range(2):
-                reb[c * FC + i, :, 8 * t : 8 * t + 8, :] = whole[:, 128 * t : 128 * t + 128].reshape(N, 8, 128)
+        if c > 0:
+            settle(c - 1)
+    take_all(pass_recv.at[CHUNKS - 1], last.at[pl.ds(0, CHIPS)])
 
     for c in sent + [fx_copy]:
         c.wait_send()
@@ -354,8 +378,29 @@
         take_all(plane_send.at[c], part_in.at[c])
         take_all(z_send.at[c], core_in.at[c])
         take_all(zb_send.at[c], core_all.at[c, pl.ds(0, 31)])
-        take_all(back_send.at[c], gathered.at[c, pl.ds(0, CHIPS - 1)])
-        take_all(pass_send.at[c], gathered.at[c, pl.ds(0, CHIPS)])
+        take_all(back_send.at[c], last.at[pl.ds(0, CHIPS - 1)])
+        take_all(pass_send.at[c], last.at[pl.ds(0, CHIPS)])
+
+
+def finish(adv, core, reb, last, lhs_out, adv_out, core_out, reb_out, final, adv_sem, core_sem, reb_sem, final_sem):
+    done = (CHUNKS - 1) * FC
+    copies = [
+        pltpu.make_async_copy(adv, adv_out, adv_sem),
+        pltpu.make_async_copy(reb, reb_out.at[pl.ds(0, done)], reb_sem),
+        pltpu.make_async_copy(core, core_out, core_sem),
+    ]
+    for c in copies:
+        c.start()
+
+    def write(i, t, values):
+        final[i, :, 8 * t : 8 * t + 8, :] = values
+        if t == 1:
+            copies.append(pltpu.make_async_copy(final.at[i], reb_out.at[done + i], final_sem.at[i]))
+            copies[-1].start()
+
+    expand(lhs_out, last, write)
+    for c in copies:
+        c.wait()
 
 
 def per_device(fields, factor_x, factor_y):
@@ -373,8 +418,8 @@
         vmem((3, 2, F, W, N, 128), f32),
         vmem((3, 2, F, W, N, 128), f32),
         vmem(whole, f32),
-        vmem((N, 128), f32),
-        vmem((N, 128), f32),
+        vmem((N, RANK), f32),
+        vmem((N, RANK), f32),
         vmem((CHUNKS, CHIPS, FC, N, 128), f32),
         vmem((CHUNKS, CHIPS - 1, FC, N, 128), f32),
         vmem((CHUNKS, RANK, FC, 128), f32),
@@ -382,35 +427,41 @@
         vmem((CHUNKS, FC, 128), f32),
         vmem((CHUNKS, RANK, FC, 128), f32),
         vmem((CHUNKS, FC, N, 128), f32),
-        vmem((CHUNKS, RANK, FC, N, 128), f32),
-        vmem((128, 256), f32),
+        vmem((CHUNKS - 1, RANK, FC, N, 128), f32),
         vmem((128, 256), f32),
         vmem((RANK, N), f32),
+        vmem((N, RANK), f32),
         dma,
+        dma((2,)),
         dma((3, 4)), dma((3, 4)), dma((2,)), dma((CHUNKS,)), dma((CHUNKS,)),
         dma((CHUNKS,)), dma((CHUNKS,)), dma((CHUNKS,)), dma((CHUNKS,)),
         dma((CHUNKS,)), dma((CHUNKS,)),
         dma((CHUNKS,)), dma((CHUNKS, CHIPS - 1)), dma((CHUNKS,)), dma((CHUNKS,)),
         pltpu.SemaphoreType.REGULAR((2, 4)),
     ]
-    advanced, core, rebuilt = pl.pallas_call(
+    inner = (whole, (F, 1, 1, 128), ((CHUNKS - 1) * FC, N, N, 128), (RANK, FC, N, 128), (128, 256))
+    kept = pl.pallas_call(
         functools.partial(kernel, rescale),
-        out_shape=(
-            jax.ShapeDtypeStruct(whole, f32),
-            jax.ShapeDtypeStruct((F, 128), f32),
-            jax.ShapeDtypeStruct(whole, f32),
-        ),
+        out_shape=[vmem(shape, f32) for shape in inner],
         in_specs=[
-            pl.BlockSpec(memory_space=pl.ANY),
-            pl.BlockSpec(memory_space=pltpu.VMEM),
-            pl.BlockSpec(memory_space=pltpu.VMEM),
+            pl.BlockSpec(memory_space=pltpu.HBM),
+            pl.BlockSpec(memory_space=pltpu.HBM),
+            pl.BlockSpec(memory_space=pltpu.HBM),
         ],
-        out_specs=[pl.BlockSpec(memory_space=pltpu.VMEM)] * 3,
+        out_specs=[pl.BlockSpec(memory_space=vmem)] * 5,
         scratch_shapes=scratch,
-        compiler_params=pltpu.CompilerParams(collective_id=0, has_side_effects=True),
+        compiler_params=pltpu.CompilerParams(collective_id=0, has_side_effects=True, vmem_limit_bytes=VMEM_BYTES),
         name="flow_tucker",
     )(fields, factor_x, factor_y)
-    return advanced, core.reshape(F, 1, 1, 128), rebuilt
+    return pl.pallas_call(
+        finish,
+        out_shape=[jax.ShapeDtypeStruct(shape, f32) for shape in (whole, (F, 1, 1, 128), whole)],
+        in_specs=[pl.BlockSpec(memory_space=vmem)] * 5,
+        out_specs=[pl.BlockSpec(memory_space=pl.ANY)] * 3,
+        scratch_shapes=[vmem((FC, N, N, 128), f32), dma, dma, dma, dma((FC,))],
+        compiler_params=pltpu.CompilerParams(vmem_limit_bytes=4 << 20),
+        name="expand_x",
+    )(*kept)
 
 
 def solution(mesh):

time: 85 us -> 79.7 us (0.938)
  local copies, waits for them, and re-layouts: 3.31 us -> 0 us
  Pallas kernels: 80.8 us -> 79 us
    unnamed x7 -> x0, local copies, waits for them, and re-layouts: 3.31 us -> none
    pallas_call x1 -> x2, Pallas kernels: 80.8 us -> 79 us  [the longest x1 77.8 us: per_device(): pl.pallas_call(functools.partial(kernel, rescale), out_shape=[vmem(shape,...]
where the time goes in v2:
time: 79.7 us; the launch traced here: 79.6 us
  Pallas kernels  79 us (99%)
    pallas_call x1, Pallas kernels, per_device(): pl.pallas_call(functools.partial(kernel, rescale), out_shape=[vmem(shape,...  77.8 us

profile of v2, /device:TPU:1, one launch (start us, length us, event | category | flops | bytes accessed | tf_op | source)
XLA Modules:
  0.0 79.6 jit_solution(9923308268662324057)
XLA Ops:
  0.6 77.8 %flow_tucker.1 = (f32[4,16,16,128]{3,2,1,0:T(8,128)S(1)}, f32[4,1,1,128]{3,2,1,0:T(1,128)S(1)}, f32[2,16,16,128]{3,2,1,0:T(8,128)S(1)}, f32[32,2,16,128]{3,2,1,0:T(8,128)S(1)}, f32[128,256]{1,0:T(8,128)S(1)}) custom-call(f32[4,16,16,128]{3,2,1,0:T(8,128)} %fields.1, f32[16,32]{1,0:T(8,128)} %fx_in.1, f32[16,32]{1,0:T(8,128)} %fy_in.1), custom_call_target="tpu_custom_call" | custom-call | tf_op jit(solution)/shard_map/flow_tucker/pallas_call | solution.py:443
  78.4 1.2 %expand_x.1 = (f32[4,16,16,128]{3,2,1,0:T(8,128)}, f32[4,1,1,128]{3,2,1,0:T(1,128)}, f32[4,16,16,128]{3,2,1,0:T(8,128)}) custom-call(f32[4,16,16,128]{3,2,1,0:T(8,128)S(1)} %get-tuple-element.8.adv, f32[4,1,1,128]{3,2,1,0:T(1,128)S(1)} %get-tuple-element.9.core, f32[2,16,16,128]{3,2,1,0:T(8,128)S(1)} %get-tuple-element.10.reb, ...), custom_call_target="tpu_custom_call" | custom-call | tf_op jit(solution)/shard_map/expand_x/pallas_call | solution.py:456

commit v3 on v2

--- a/solution.py
+++ b/solution.py
@@ -107,8 +107,9 @@
     def take_all(sem, ref):
         pltpu.make_async_copy(ref, ref, sem).wait()
 
-    load = pltpu.make_async_copy(fields, state.at[0], load_sem)
-    load.start()
+    loads = [pltpu.make_async_copy(fields.at[f], state.at[0, f], load_sem.at[f]) for f in range(F)]
+    for c in loads:
+        c.start()
     factors = [
         pltpu.make_async_copy(fx_in, fx_own, factor_sems.at[0]),
         pltpu.make_async_copy(fy_in, fy, factor_sems.at[1]),
@@ -144,24 +145,28 @@
     for c in factors:
         c.wait()
     fx_copy.start()
-    load.wait()
 
     def flat(s):
         return (adv if s == 3 else state.at[s]).reshape(F * N * N, 128)
 
+    def send_edges(s, f):
+        now = state.at[s, f]
+        for k, (src, dst, axis, step) in enumerate((
+            (edge_y.at[s, LOW, f], halo_y.at[s, TOP, f], "gy", -1),
+            (edge_y.at[s, TOP, f], halo_y.at[s, LOW, f], "gy", 1),
+            (now.at[pl.ds(0, W)], halo_x.at[s, TOP, f], "gx", -1),
+            (now.at[pl.ds(N - W, W)], halo_x.at[s, LOW, f], "gx", 1),
+        )):
+            copy(src, dst, halo_send.at[s, k], halo_recv.at[s, k], along(axis, step)).start()
+
     for f in range(F):
+        loads[f].wait()
         for j in range(W):
             edge_y[0, LOW, f, j] = flat(0)[pl.ds(f * N * N + j, N, stride=N), :]
             edge_y[0, TOP, f, j] = flat(0)[pl.ds(f * N * N + N - W + j, N, stride=N), :]
-
-    def halo_copies(s):
-        now = state.at[s]
-        return (
-            copy(edge_y.at[s, LOW], halo_y.at[s, TOP], halo_send.at[s, 0], halo_recv.at[s, 0], along("gy", -1)),
-            copy(edge_y.at[s, TOP], halo_y.at[s, LOW], halo_send.at[s, 1], halo_recv.at[s, 1], along("gy", 1)),
-            copy(now.at[:, pl.ds(0, W)], halo_x.at[s, TOP], halo_send.at[s, 2], halo_recv.at[s, 2], along("gx", -1)),
-            copy(now.at[:, pl.ds(N - W, W)], halo_x.at[s, LOW], halo_send.at[s, 3], halo_recv.at[s, 3], along("gx", 1)),
-        )
+        if f:
+            send_edges(0, f - 1)
+    send_edges(0, F - 1)
 
     def fluxes(values, which):
         total = [values[which] * v for v in values]
@@ -178,14 +183,17 @@
         lhs_out[...] = rescale * spread(rows, RANK)
         fy_t[...] = dot(one_hot(iota((RANK, RANK), 0) == iota((RANK, RANK), 1)), fy[...], ((1,), (1,)))
 
+    def hand_on(s, f):
+        if s < 2:
+            send_edges(s + 1, f)
+        else:
+            mates.append(copy(adv.at[f], mate_adv.at[f], mate_send.at[f], mate_recv.at[f], mate))
+            mates[-1].start()
+
     def section(s):
         keep, take = SECTIONS[s]
         now, base = state.at[s], state.at[0]
         after = adv if s == 2 else state.at[s + 1]
-        copies = halo_copies(s)
-        for c in copies:
-            c.start()
-
         @pl.loop(0, N)
         def _(x):
             for t in range(2):
@@ -229,8 +237,8 @@
             sign_in(s + 1)
         if s == 1:
             prepare()
-        copies[2].wait_recv()
-        copies[3].wait_recv()
+        take_all(halo_recv.at[s, 2], halo_x.at[s, TOP])
+        take_all(halo_recv.at[s, 3], halo_x.at[s, LOW])
         for side, first in ((LOW, 0), (TOP, N + W)):
             @pl.loop(0, W)
             def _(j):
@@ -248,8 +256,8 @@
         if s == 1:
             signed_in(2)
             sign_in(3)
-        copies[0].wait_recv()
-        copies[1].wait_recv()
+        take_all(halo_recv.at[s, 0], halo_y.at[s, TOP])
+        take_all(halo_recv.at[s, 1], halo_y.at[s, LOW])
         out = flat(s + 1)
         flux = []
         for side, near in ((LOW, (2, 1, 0)), (TOP, (0, 1, 2))):
@@ -270,21 +278,15 @@
                     out[at, :] = new
                     if s < 2:
                         edge_y[s + 1, side, f, k if side == LOW else W - 1 - k] = new
-            if s == 2 and (f + 1) % FC == 0:
-                c = f // FC
-                piece = pl.ds(c * FC, FC)
-                mates.append(copy(adv.at[piece], mate_adv.at[piece], mate_send.at[c], mate_recv.at[c], mate))
-                mates[-1].start()
-        return copies
+            if f:
+                hand_on(s, f - 1)
+        hand_on(s, F - 1)
 
     mates = []
-    sent = []
-    sent += section(0)
-    sent += section(1)
-    sent += section(2)
+    for s in range(3):
+        section(s)
 
     signed_in(3)
-    sent += mates
 
     def tiles(ref, f):
         return jnp.concatenate(
@@ -292,21 +294,20 @@
         )
 
     chip = gx // 2
-    plane = []
-    for c in range(CHUNKS):
-        mates[c].wait_recv()
+    for c in range(CHUNKS):
         for i in range(FC):
             f = c * FC + i
+            mates[f].wait_recv()
             both = jnp.concatenate([tiles(adv, f), tiles(mate_adv, f)], axis=0)
             total = dot(lhs_in[...], both)
             for t in range(2):
                 part[c, :, i, 8 * t : 8 * t + 8, :] = total[:, 128 * t : 128 * t + 128].reshape(CHIPS, 8, 128)
-        for k in PLANE_ORDER:
-            to = lax.rem(chip + k, CHIPS)
-            plane.append(
-                copy(part.at[c, to], part_in.at[c, k - 1], plane_send.at[c], plane_recv.at[c], {"gx": 2 * to + core})
-            )
-            plane[-1].start()
+            for k in PLANE_ORDER:
+                to = lax.rem(chip + k, CHIPS)
+                copy(
+                    part.at[c, to, i], part_in.at[c, k - 1, i], plane_send.at[c], plane_recv.at[c],
+                    {"gx": 2 * to + core},
+                ).start()
 
     out_z = []
     for c in range(CHUNKS):
@@ -372,8 +373,11 @@
             settle(c - 1)
     take_all(pass_recv.at[CHUNKS - 1], last.at[pl.ds(0, CHIPS)])
 
-    for c in sent + [fx_copy]:
+    for c in mates + [fx_copy]:
         c.wait_send()
+    for s in range(3):
+        for k in range(4):
+            take_all(halo_send.at[s, k], halo_y.at[s, k // 2])
     for c in range(CHUNKS):
         take_all(plane_send.at[c], part_in.at[c])
         take_all(z_send.at[c], core_in.at[c])
@@ -431,9 +435,9 @@
         vmem((128, 256), f32),
         vmem((RANK, N), f32),
         vmem((N, RANK), f32),
-        dma,
+        dma((F,)),
         dma((2,)),
-        dma((3, 4)), dma((3, 4)), dma((2,)), dma((CHUNKS,)), dma((CHUNKS,)),
+        dma((3, 4)), dma((3, 4)), dma((2,)), dma((F,)), dma((F,)),
         dma((CHUNKS,)), dma((CHUNKS,)), dma((CHUNKS,)), dma((CHUNKS,)),
         dma((CHUNKS,)), dma((CHUNKS,)),
         dma((CHUNKS,)), dma((CHUNKS, CHIPS - 1)), dma((CHUNKS,)), dma((CHUNKS,)),

time: 79.7 us -> 80 us (level)
  no operation moved by 1% of the time
where the time goes in v3:
time: 80 us; the launch traced here: 79.8 us
  Pallas kernels  79.2 us (99%)
    pallas_call x1, Pallas kernels, per_device(): pl.pallas_call(functools.partial(kernel, rescale), out_shape=[vmem(shape,...  78 us

profile of v3, /device:TPU:1, one launch (start us, length us, event | category | flops | bytes accessed | tf_op | source)
XLA Modules:
  0.0 79.8 jit_solution(8658999954933411194)
XLA Ops:
  0.6 78.0 %flow_tucker.1 = (f32[4,16,16,128]{3,2,1,0:T(8,128)S(1)}, f32[4,1,1,128]{3,2,1,0:T(1,128)S(1)}, f32[2,16,16,128]{3,2,1,0:T(8,128)S(1)}, f32[32,2,16,128]{3,2,1,0:T(8,128)S(1)}, f32[128,256]{1,0:T(8,128)S(1)}) custom-call(f32[4,16,16,128]{3,2,1,0:T(8,128)} %fields.1, f32[16,32]{1,0:T(8,128)} %fx_in.1, f32[16,32]{1,0:T(8,128)} %fy_in.1), custom_call_target="tpu_custom_call" | custom-call | tf_op jit(solution)/shard_map/flow_tucker/pallas_call | solution.py:447
  78.6 1.2 %expand_x.1 = (f32[4,16,16,128]{3,2,1,0:T(8,128)}, f32[4,1,1,128]{3,2,1,0:T(1,128)}, f32[4,16,16,128]{3,2,1,0:T(8,128)}) custom-call(f32[4,16,16,128]{3,2,1,0:T(8,128)S(1)} %get-tuple-element.8.adv, f32[4,1,1,128]{3,2,1,0:T(1,128)S(1)} %get-tuple-element.9.core, f32[2,16,16,128]{3,2,1,0:T(8,128)S(1)} %get-tuple-element.10.reb, ...), custom_call_target="tpu_custom_call" | custom-call | tf_op jit(solution)/shard_map/expand_x/pallas_call | solution.py:460
